TPU v7x, 32 devices: a whole 2x2x4 slice. The times are simulated.
32 devices in a mesh: rep: 4 (over y, core), tp: 8 (over z, x).
Axes of the slice: x: 2, y: 2, z: 4, core: 2. Of those that a mesh axis runs over, the one named last changes fastest.
Arguments:
- tokens: bfloat16 [2560, 5120], P(('rep', 'tp')), parts along dimension 0
- weights: bfloat16 [3, 5120, 4096], P(None, None, 'tp')
- modulation: float32 [2, 36, 5120], P(None, 'rep'), parts along dimension 1, may hold values from -3 to 3
- qk_gain: float32 [2, 4096], P(None, 'tp'), may hold values from 0.25 to 1.75
- segment_ids: int32 [2560], P('rep'), parts along dimension 0, may hold values from 0 to 9, as said below
- positions: int32 [3, 2560], P(None, 'rep'), parts along dimension 1, may hold values from 0 to 15, as said below
- page_table: int32 [160], P('rep'), parts along dimension 0, may hold values from 0 to 79, as said below
- kv_cache: bfloat16 [2, 32, 320, 16, 128], P(None, 'tp', 'rep'), parts along dimension 2, may hold values from -6 to 6
Outputs:
- attended: bfloat16 [2560, 4096], P(('rep', 'tp')), parts along dimension 0
- new_cache: bfloat16 [2, 32, 320, 16, 128], P(None, 'tp', 'rep'), parts along dimension 2
There are 4 independent parts, one for each index of `rep`. A program takes and returns all parts, laid end to end along the dimension named above; an argument that names none is the same for every part. Nothing has to cross between parts.
Inputs may be any that keep to these rules, and one draw needn't show every extreme that they name: `segment_ids`: never falling; 0 on the first 512 tokens (the long clip); then clips 1 to 8 in order, each of 8 to 16 tokens, at least one of exactly 16; the remaining tokens are padding with id 9. `positions`: each token's frame, height and width index on its clip's grid; 0 on padding tokens. `page_table`: distinct pages.
All inputs are finite; a program needn't handle non-finite values.
Results may differ from a plain program's by a relative error of at most 0.0047.
Values may be sent and summed in bfloat16 or wider, within the bound.
No kernel may reach another device: no remote copies, remote signals or barrier semaphores. Data moves between devices by JAX's collectives and lax.ppermute only.
A program may use at most 128 MiB of HBM per device.

v0:
```python
import math
import jax
import jax.numpy as jnp
import numpy as np
from jax import lax
from jax.sharding import PartitionSpec as P

HEAD = 128
HEADS = 32
PAGE = 16
epsilon = 1e-06
masked_score = -1e30


def rotary_tables(positions, head_size):
    height_dims = 2 * (head_size // 6)
    frame_dims = head_size - 2 * height_dims
    frame_freq = 1.0 / 10000.0 ** (np.arange(0, frame_dims, 2) / frame_dims)
    height_freq = 1.0 / 10000.0 ** (np.arange(0, height_dims, 2) / height_dims)
    zero_frame = np.zeros(frame_dims // 2)
    zero_height = np.zeros(height_dims // 2)
    table_frame = np.concatenate([frame_freq, zero_height, zero_height])
    table_height = np.concatenate([zero_frame, height_freq, zero_height])
    table_width = np.concatenate([zero_frame, zero_height, height_freq])
    coords = positions.astype(jnp.float32)
    angles = coords[0][:, None] * jnp.asarray(table_frame, jnp.float32)[None, :]
    angles = angles + coords[1][:, None] * jnp.asarray(table_height, jnp.float32)[None, :]
    angles = angles + coords[2][:, None] * jnp.asarray(table_width, jnp.float32)[None, :]
    return (jnp.cos(angles), jnp.sin(angles))


def rotary_apply(channels, cosine, sine_table):
    first = channels[..., 0::2]
    second = channels[..., 1::2]
    cos_rows = cosine[:, None, :]
    sin_rows = sine_table[:, None, :]
    turned = jnp.stack(
        [first * cos_rows - second * sin_rows, first * sin_rows + second * cos_rows], axis=-1
    )
    return turned.reshape(channels.shape)


def layer_norm_mod(rows, seg_rows, modulation):
    floats = rows.astype(jnp.float32)
    center = floats - jnp.mean(floats, axis=1, keepdims=True)
    spread = jnp.mean(center * center, axis=1, keepdims=True)
    normed = center * lax.rsqrt(spread + epsilon)
    onehot = (
        seg_rows[:, None] == jnp.arange(modulation.shape[1], dtype=jnp.int32)[None, :]
    ).astype(jnp.float32)
    shifts = jnp.dot(onehot, modulation[0], precision=lax.Precision.HIGHEST)
    scales = jnp.dot(onehot, modulation[1], precision=lax.Precision.HIGHEST)
    return (normed * (1.0 + scales) + shifts).astype(jnp.bfloat16)


def attend_block(q_block, key_all, value_all, seg_query, seg_keys, clip_count):
    scaling = float(q_block.shape[2]) ** (-0.5)
    scores = (
        jnp.einsum("qhd,khd->hqk", q_block, key_all, preferred_element_type=jnp.float32) * scaling
    )
    query_live = seg_query < clip_count
    allowed = (seg_query[:, None] == seg_keys[None, :]) & query_live[:, None]
    scores = jnp.where(allowed[None], scores, masked_score)
    row_top = jnp.max(scores, axis=2, keepdims=True)
    exponent = jnp.exp(scores - row_top)
    row_total = jnp.sum(exponent, axis=2)
    probabilities = exponent.astype(jnp.bfloat16)
    result = jnp.einsum(
        "hqk,khd->qhd", probabilities, value_all, preferred_element_type=jnp.float32
    )
    result = result / row_total.T[:, :, None]
    return jnp.where(query_live[:, None, None], result, 0.0).astype(jnp.bfloat16)


def attend_range(q_rot, k_rot, v_low, segment_ids, clip_count, row_low, row_high):
    block_rows = math.gcd(row_high - row_low, 512)
    results = []
    for row_start in range(row_low, row_high, block_rows):
        q_block = q_rot[row_start : row_start + block_rows]
        seg_query = segment_ids[row_start : row_start + block_rows]
        results.append(attend_block(q_block, k_rot, v_low, seg_query, segment_ids, clip_count))
    return jnp.concatenate(results, axis=0)


def body(tokens, weights, modulation, qk_gain, segment_ids, positions, page_table, kv_cache):
    tok_rows = tokens.shape[0]
    head_here = weights.shape[2] // HEAD
    self_rank = lax.axis_index("tp")
    own_seg = lax.dynamic_slice_in_dim(segment_ids, self_rank * tok_rows, tok_rows)
    x_mod = layer_norm_mod(tokens, own_seg, modulation)
    projected = jnp.einsum(
        "td,cdh->tch",
        lax.all_gather(x_mod, "tp", axis=0, tiled=True),
        weights,
        preferred_element_type=jnp.float32,
    )
    total_rows = projected.shape[0]
    queries = projected[:, 0]
    key_rows = projected[:, 1]
    values = projected[:, 2]
    q_part = jnp.sum(queries * queries, axis=1)
    k_part = jnp.sum(key_rows * key_rows, axis=1)
    q_total, k_total = lax.psum((q_part, k_part), "tp")
    channels = HEADS * HEAD
    q_mean = q_total / channels
    k_mean = k_total / channels
    cosine, sine_table = rotary_tables(positions, HEAD)
    q_norm = queries * lax.rsqrt(q_mean + epsilon)[:, None] * qk_gain[0][None, :]
    k_norm = key_rows * lax.rsqrt(k_mean + epsilon)[:, None] * qk_gain[1][None, :]
    q_rot = rotary_apply(q_norm.reshape(total_rows, head_here, HEAD), cosine, sine_table).astype(
        jnp.bfloat16
    )
    k_rot = rotary_apply(k_norm.reshape(total_rows, head_here, HEAD), cosine, sine_table).astype(
        jnp.bfloat16
    )
    v_low = values.astype(jnp.bfloat16).reshape(total_rows, head_here, HEAD)
    clip_count = modulation.shape[1]
    heads_out = attend_range(q_rot, k_rot, v_low, segment_ids, clip_count, 0, total_rows)
    local_heads = heads_out.reshape(total_rows, head_here * HEAD)
    attended = lax.all_to_all(local_heads, "tp", split_axis=0, concat_axis=1, tiled=True)
    page_count = total_rows // PAGE
    stacked = jnp.stack([k_rot, v_low]).reshape(2, page_count, PAGE, head_here, HEAD)
    paged = stacked.transpose(0, 3, 1, 2, 4)
    new_cache = kv_cache.at[:, :, page_table].set(paged)
    return (attended, new_cache)


def solution(mesh):
    return jax.shard_map(
        body,
        mesh=mesh,
        in_specs=(
            P(("rep", "tp"), None),
            P(None, None, "tp"),
            P(None, "rep", None),
            P(None, "tp"),
            P("rep"),
            P(None, "rep"),
            P("rep"),
            P(None, "tp", "rep", None, None),
        ),
        out_specs=(P(("rep", "tp"), None), P(None, "tp", "rep", None, None)),
        check_vma=False,
    )
```

profile of v0, /device:TPU:0, one launch (start us, length us, event | category | flops | bytes accessed | tf_op | source)
XLA Modules:
  0.0 209.8 jit_solution(9179816247852573089)
XLA Ops:
  7.2 1.1 copy-done
  9.3 1.0 fusion.2
  10.4 1.7 fusion.3
  12.3 1.4 fusion.55
  13.7 1.0 compare_and_fusion
  14.7 102.2 %all-gather.2.cloned.1.call-done = bf16[640,5120]{1,0:T(8,128)(2,1)} async-done(((bf16[80,5120]{1,0:T(8,128)(2,1)}), bf16[640,5120]{1,0:T(8,128)(2,1)}) %all-gather.2.cloned.1.call-update) | async-done | bytes 6553616 | tf_op jit(solution)/shard_map/all_gather | solution.py:93
  116.9 16.9 %fusion = f32[640,3,512]{0,2,1:T(8,128)S(1)} fusion(bf16[3,5120,512]{2,1,0:T(8,128)(2,1)} %param.12, bf16[640,5120]{1,0:T(8,128)(2,1)} %all-gather.2.cloned.1.call-done), kind=kOutput, calls=%fused_computation.1 | convolution fusion | flops 10066329600 | bytes 26214400 | tf_op jit(solution)/shard_map/td,cdh->tch/dot_general | solution.py:91
  134.3 19.0 %all-reduce = (f32[640]{0:T(1024)S(1)}, f32[640]{0:T(1024)S(1)}) all-reduce(f32[640]{0:T(1024)S(1)} %get-tuple-element.3, f32[640]{0:T(1024)S(1)} %get-tuple-element.2), channel_id=1, replica_groups=mesh['rep'=4,'tp'=8] {'tp'}, use_global_device_ids=true, to_apply=%region_3.0 | all-reduce | flops 1280 | bytes 10240 | tf_op jit(solution)/shard_map/psum | solution.py:103
  153.3 1.2 multiply_multiply_fusion.1
  154.5 3.4 %slice.97 = f32[640,4,64]{0,2,1:T(8,128)} slice(f32[640,4,128]{0,2,1:T(8,128)} %multiply_multiply_fusion.1), slice={[0:640:1], [0:4:1], [1:128:2]} | slice | bytes 1310720 | tf_op jit(solution)/shard_map/slice | solution.py:34
  158.0 1.5 slice.93
  160.3 1.5 fusion.53
  161.8 0.9 pad_maximum_fusion
  162.7 0.8 copy.88
  164.0 0.5 copy.89
  164.5 1.4 maximum_convert_fusion
  165.9 0.8 copy.90
  166.8 0.8 copy.92
  168.3 0.5 fusion.65
  170.1 0.5 fusion.66
  171.9 0.5 fusion.67
  173.7 0.5 fusion.68
  175.1 0.5 fusion.69
  176.4 0.5 copy.110
  177.0 1.1 all_to_all.14
  178.1 4.2 %all-to-all-start = ((bf16[8,80,512]{2,1,0:T(8,128)(2,1)}), bf16[8,80,512]{2,1,0:T(8,128)(2,1)}, u32[]{:S(2)}, u32[]{:S(2)}) async-start(bf16[8,80,512]{2,1,0:T(8,128)(2,1)} %all_to_all.14), calls=%async_computation | async-start | bytes 1310720 | tf_op jit(solution)/shard_map/all_to_all | solution.py:120
  182.6 5.0 %convert_element_type.94 = bf16[1,40,16,4,128]{2,1,4,3,0:T(8,128)(2,1)} reshape(bf16[640,4,64,2]{0,3,2,1:T(2,128)(2,1)S(1)} %maximum_convert_fusion) | data formatting | bytes 1310720 | tf_op jit(solution)/shard_map/convert_element_type | solution.py:113
  187.9 4.6 %copy.113 = bf16[1,40,16,4,128]{4,2,3,1,0:T(8,128)(2,1)S(1)} copy(bf16[1,40,16,4,128]{2,1,4,3,0:T(8,128)(2,1)} %convert_element_type.94) | data formatting | bytes 1310720 | tf_op jit(solution)/shard_map/convert_element_type | solution.py:113
  192.6 1.3 copy.115
  193.9 0.9 copy-done.2
  194.8 5.6 %scatter_fusion = bf16[2,4,80,16,128]{4,3,2,1,0:T(8,128)(2,1)S(1)} fusion(bf16[2,4,80,16,128]{4,3,2,1,0:T(8,128)(2,1)S(1)} %copy-done.2, s32[40]{0:T(128)S(1)} %compare_select_fusion, bf16[40,2,4,16,128]{4,3,2,1,0:T(8,128)(2,1)} %copy.115), kind=kCustom, calls=%fused_computation | custom fusion | bytes 3932320 | tf_op jit(solution)/shard_map/scatter | solution.py:124
  200.4 2.5 %copy.129 = bf16[8,10,8,512]{3,2,0,1:T(8,128)(2,1)} copy(bf16[8,10,8,512]{3,2,1,0:T(8,128)(2,1)} %bitcast.29) | data formatting | bytes 1310720 | tf_op jit(solution)/shard_map/all_to_all | solution.py:120
  (95 shorter events, 9.5 us)
Async XLA Ops:
  7.2 1.1 copy-start
  7.2 109.7 %all-gather.2.cloned.1.call-start = ((), (), s32[]{:S(2)}) async-start(), calls=%async_computation.1 | async-start | bytes 7372800 | tf_op jit(solution)/shard_map/all_gather | solution.py:93
  7.2 1.7 copy-start.10
  7.2 2.0 copy-start.15
  10.3 1.8 copy-start.16
  10.3 1.9 copy-start.17
  10.3 2.0 copy-start.24
  10.4 1.9 copy-start.25
  10.4 1.9 copy-start.26
  12.3 121.6 %copy-start.18 = (pred[128]{0:T(512)(128)(4,1)}, pred[128]{0:T(512)(128)(4,1)S(1)}, u32[]{:S(2)}) copy-start(pred[128]{0:T(512)(128)(4,1)S(1)} %get-tuple-element.32) | copy-start | bytes 388
  12.3 121.6 %copy-start.20 = (pred[128]{0:T(512)(128)(4,1)}, pred[128]{0:T(512)(128)(4,1)S(1)}, u32[]{:S(2)}) copy-start(pred[128]{0:T(512)(128)(4,1)S(1)} %get-tuple-element.31) | copy-start | bytes 388
  12.3 121.6 %copy-start.22 = (pred[128]{0:T(512)(128)(4,1)}, pred[128]{0:T(512)(128)(4,1)S(1)}, u32[]{:S(2)}) copy-start(pred[128]{0:T(512)(128)(4,1)S(1)} %get-tuple-element.30) | copy-start | bytes 388
  154.5 3.5 %copy-start.3 = (f32[640,4,128]{0,2,1:T(8,128)S(1)}, f32[640,4,128]{0,2,1:T(8,128)}, u32[]{:S(2)}) copy-start(f32[640,4,128]{0,2,1:T(8,128)} %multiply_multiply_fusion.1) | copy-start | bytes 3932164
  161.8 1.7 copy-start.4
  165.9 1.7 copy-start.9
  165.9 1.9 copy-start.8
  165.9 2.0 copy-start.7
  166.8 1.3 copy-start.6
  166.8 1.4 copy-start.5
  166.8 1.4 copy-start.14
  168.3 0.9 copy-start.23
  169.2 0.9 copy-start.13
  170.1 0.9 copy-start.21
  171.0 0.9 copy-start.12
  171.9 0.9 copy-start.19
  172.8 0.9 copy-start.11
  177.0 5.3 %copy-start.27 = (s32[40]{0:T(128)S(1)}, s32[40]{0:T(128)}, u32[]{:S(2)}) copy-start(s32[40]{0:T(128)} %param.17) | copy-start | bytes 484
  178.1 22.4 %all-to-all-start = ((bf16[8,80,512]{2,1,0:T(8,128)(2,1)}), bf16[8,80,512]{2,1,0:T(8,128)(2,1)}, u32[]{:S(2)}, u32[]{:S(2)}) async-start(bf16[8,80,512]{2,1,0:T(8,128)(2,1)} %all_to_all.14), calls=%async_computation | async-start | bytes 1310720 | tf_op jit(solution)/shard_map/all_to_all | solution.py:120
  192.6 2.2 %copy-start.2 = (bf16[2,4,80,16,128]{4,3,2,1,0:T(8,128)(2,1)S(1)}, bf16[2,4,80,16,128]{4,3,2,1,0:T(8,128)(2,1)}, u32[]{:S(2)}) copy-start(bf16[2,4,80,16,128]{4,3,2,1,0:T(8,128)(2,1)} %param.18) | copy-start | bytes 7864324
  200.4 2.5 %copy-start.1 = (bf16[2,4,80,16,128]{4,3,2,1,0:T(8,128)(2,1)}, bf16[2,4,80,16,128]{4,3,2,1,0:T(8,128)(2,1)S(1)}, u32[]{:S(2)}) copy-start(bf16[2,4,80,16,128]{4,3,2,1,0:T(8,128)(2,1)S(1)} %scatter_fusion) | copy-start | bytes 7864324
Sparse Core Ops, SparseCore 0:
  12.3 104.5 all-gather.1
where the time goes:
time: 210 us
  waiting for transfers between devices  102 us (49%)
  local copies, waits for them, and re-layouts  34.4 us (16%)
  matrix products  24.6 us (12%)
  blocking collectives  19 us (9%)
  between operations  14.7 us (7%)
  other arithmetic  10.6 us (5%)
  starting transfers between devices  4.25 us (2%)
    all_gather x1, waiting for transfers between devices, body(): lax.all_gather(x_mod, 'tp', axis=0, tiled=True)  102 us
    psum x1, blocking collectives, body(): q_total, k_total = lax.psum((q_part, k_part), 'tp')  19 us
    dot_general x1, matrix products, body(): jnp.einsum('td,cdh->tch', lax.all_gather(x_mod, 'tp', axis=0, tiled=True)...  16.9 us
    convert_element_type x4, local copies, waits for them, and re-layouts, body(): rotary_apply(k_norm.reshape(total_rows, head_here, HEAD), cosine, sine_ta...  11.3 us
    scatter x1, local copies, waits for them, and re-layouts, body(): new_cache = kv_cache.at[:, :, page_table].set(paged)  5.59 us
    all_to_all x1, starting transfers between devices, body(): lax.all_to_all(local_heads, 'tp', split_axis=0, concat_axis=1, tiled=True)  4.21 us
  transfers between devices with their start and end apart: 2, of which 1 were waited for; matrix products, arithmetic and copies ran while one was open for 9% of the time, Pallas kernels for 0%

commit v1 on v0

--- a/solution.py
+++ b/solution.py
@@ -88,12 +88,21 @@
     self_rank = lax.axis_index("tp")
     own_seg = lax.dynamic_slice_in_dim(segment_ids, self_rank * tok_rows, tok_rows)
     x_mod = layer_norm_mod(tokens, own_seg, modulation)
-    projected = jnp.einsum(
-        "td,cdh->tch",
-        lax.all_gather(x_mod, "tp", axis=0, tiled=True),
-        weights,
-        preferred_element_type=jnp.float32,
-    )
+    ways, here, lap = (lax.axis_size("tp"), lax.axis_index("tp"), x_mod.shape[0])
+    earlier, later = ([], [])
+    going_up = going_down = x_mod
+    for far in range(ways // 2 + 1):
+        earlier.append(
+            jnp.einsum("td,cdh->tch", going_up, weights, preferred_element_type=jnp.float32)
+        )
+        if 0 < far < ways - ways // 2:
+            later.append(
+                jnp.einsum("td,cdh->tch", going_down, weights, preferred_element_type=jnp.float32)
+            )
+        going_up = lax.ppermute(going_up, "tp", [(d, (d + 1) % ways) for d in range(ways)])
+        going_down = lax.ppermute(going_down, "tp", [(d, (d - 1) % ways) for d in range(ways)])
+    line = jnp.concatenate([*earlier[::-1], *later], axis=0)
+    projected = jnp.roll(line, (here - ways // 2) * earlier[0].shape[0], axis=0)
     total_rows = projected.shape[0]
     queries = projected[:, 0]
     key_rows = projected[:, 1]

time: 210 us -> 245 us (1.17); the launches traced: 210 us -> 241 us
  starting transfers between devices: 4.25 us -> 51.3 us
  waiting for transfers between devices: 102 us -> 81.2 us
  matrix products: 24.6 us -> 38 us
  between operations: 14.7 us -> 1.54 us
  local copies, waits for them, and re-layouts: 34.4 us -> 37.1 us
    all_gather x1 -> x0, waiting for transfers between devices: 102 us -> none  [body(): lax.all_gather(x_mod, 'tp', axis=0, tiled=True)]
    ppermute x0 -> x7, waiting for transfers between devices: none -> 81.2 us  [the longest x4 81.2 us: body(): lax.ppermute(going_up, 'tp', [(d, (d + 1) % ways) for d in range(ways)])]
    ppermute x0 -> x7, starting transfers between devices: none -> 47.7 us  [the longest x3 39.6 us: body(): lax.ppermute(going_down, 'tp', [(d, (d - 1) % ways) for d in range(ways)])]
    dot_general x1 -> x8, matrix products: 16.9 us -> 31.1 us  [the longest x5 21.1 us: body(): jnp.einsum('td,cdh->tch', going_up, weights, preferred_element_type=jnp.f...]
  transfers between devices with their start and end apart: 2 -> 8, of which waited for: 1 -> 4; matrix products, arithmetic and copies ran while one was open for 9% -> 20% of each run, Pallas kernels for 0% -> 0%
where the time goes in v1:
time: 245 us; the launch traced here: 241 us
  waiting for transfers between devices  81.2 us (33%)
  starting transfers between devices  51.3 us (21%)
  matrix products  38 us (16%)
  local copies, waits for them, and re-layouts  37.1 us (15%)
  blocking collectives  19.9 us (8%)
  other arithmetic  11.6 us (5%)
    ppermute x4, waiting for transfers between devices, body(): lax.ppermute(going_up, 'tp', [(d, (d + 1) % ways) for d in range(ways)])  81.2 us
    ppermute x3, starting transfers between devices, body(): lax.ppermute(going_down, 'tp', [(d, (d - 1) % ways) for d in range(ways)])  39.6 us
    dot_general x5, matrix products, body(): jnp.einsum('td,cdh->tch', going_up, weights, preferred_element_type=jnp.f...  21.1 us
    psum x1, blocking collectives, body(): q_total, k_total = lax.psum((q_part, k_part), 'tp')  19.9 us
    convert_element_type x4, local copies, waits for them, and re-layouts, body(): rotary_apply(k_norm.reshape(total_rows, head_here, HEAD), cosine, sine_ta...  11.4 us
    dot_general x3, matrix products, body(): jnp.einsum('td,cdh->tch', going_down, weights, preferred_element_type=jnp...  9.92 us
    ppermute x4, starting transfers between devices, body(): lax.ppermute(going_up, 'tp', [(d, (d + 1) % ways) for d in range(ways)])  8.09 us
    scatter x1, local copies, waits for them, and re-layouts, body(): new_cache = kv_cache.at[:, :, page_table].set(paged)  5.59 us
  transfers between devices with their start and end apart: 8, of which 4 were waited for; matrix products, arithmetic and copies ran while one was open for 20% of the time, Pallas kernels for 0%

profile of v1, /device:TPU:0, one launch (start us, length us, event | category | flops | bytes accessed | tf_op | source)
XLA Modules:
  0.0 240.6 jit_solution(13034465556995018366)
XLA Ops:
  4.5 3.0 %collective-permute-start = (bf16[80,5120]{1,0:T(8,128)(2,1)S(1)}, bf16[80,5120]{1,0:T(8,128)(2,1)S(1)}, u32[]{:S(2)}, u32[]{:S(2)}) collective-permute-start(bf16[80,5120]{1,0:T(8,128)(2,1)S(1)} %fusion.1), channel_id=1, source_target_pairs={{0,1},{1,2},{2,3},{3,4},{4,5},{5,6},{6,7},{7,0},{8,9},{9,10},{10,1... | collective-permute-start | bytes 2457608 | tf_op jit(solution)/shard_map/ppermute | solution.py:102
  7.6 21.3 %collective-permute-done = bf16[80,5120]{1,0:T(8,128)(2,1)S(1)} collective-permute-done((bf16[80,5120]{1,0:T(8,128)(2,1)S(1)}, bf16[80,5120]{1,0:T(8,128)(2,1)S(1)}, u32[]{:S(2)}, u32[]{:S(2)}) %collective-permute-start) | collective-permute-done | bytes 819232 | tf_op jit(solution)/shard_map/ppermute | solution.py:102
  28.9 4.7 %collective-permute-start.4 = (bf16[80,5120]{1,0:T(8,128)(2,1)S(1)}, bf16[80,5120]{1,0:T(8,128)(2,1)S(1)}, u32[]{:S(2)}, u32[]{:S(2)}) collective-permute-start(bf16[80,5120]{1,0:T(8,128)(2,1)S(1)} %fusion.1), channel_id=1, source_target_pairs={{0,7},{1,0},{2,1},{3,2},{4,3},{5,4},{6,5},{7,6},{8,15},{9,8},{10,9... | collective-permute-start | bytes 2457608 | tf_op jit(solution)/shard_map/ppermute | solution.py:103
  33.6 30.0 %collective-permute-done.1 = bf16[80,5120]{1,0:T(8,128)(2,1)S(1)} collective-permute-done((bf16[80,5120]{1,0:T(8,128)(2,1)S(1)}, bf16[80,5120]{1,0:T(8,128)(2,1)S(1)}, u32[]{:S(2)}, u32[]{:S(2)}) %collective-permute-start.1) | collective-permute-done | bytes 819232 | tf_op jit(solution)/shard_map/ppermute | solution.py:102
  63.6 2.5 %collective-permute-start.2 = (bf16[80,5120]{1,0:T(8,128)(2,1)S(1)}, bf16[80,5120]{1,0:T(8,128)(2,1)}, u32[]{:S(2)}, u32[]{:S(2)}) collective-permute-start(bf16[80,5120]{1,0:T(8,128)(2,1)S(1)} %collective-permute-done.1), channel_id=1, source_target_pairs={{0,1},{1,2},{2,3},{3,4},{4,5},{5,6},{6,7},{7,0},{8,9},{9,10},{10,1... | collective-permute-start | bytes 2457608 | tf_op jit(solution)/shard_map/ppermute | solution.py:102
  66.1 18.6 %collective-permute-start.5 = (bf16[80,5120]{1,0:T(8,128)(2,1)S(1)}, bf16[80,5120]{1,0:T(8,128)(2,1)}, u32[]{:S(2)}, u32[]{:S(2)}) collective-permute-start(bf16[80,5120]{1,0:T(8,128)(2,1)S(1)} %collective-permute-done.4), channel_id=1, source_target_pairs={{0,7},{1,0},{2,1},{3,2},{4,3},{5,4},{6,5},{7,6},{8,15},{9,8},{10,9... | collective-permute-start | bytes 2457608 | tf_op jit(solution)/shard_map/ppermute | solution.py:103
  84.7 15.5 %collective-permute-done.2 = bf16[80,5120]{1,0:T(8,128)(2,1)} collective-permute-done((bf16[80,5120]{1,0:T(8,128)(2,1)S(1)}, bf16[80,5120]{1,0:T(8,128)(2,1)}, u32[]{:S(2)}, u32[]{:S(2)}) %collective-permute-start.2) | collective-permute-done | bytes 819232 | tf_op jit(solution)/shard_map/ppermute | solution.py:102
  100.1 2.6 %collective-permute-start.3 = (bf16[80,5120]{1,0:T(8,128)(2,1)}, bf16[80,5120]{1,0:T(8,128)(2,1)}, u32[]{:S(2)}, u32[]{:S(2)}) collective-permute-start(bf16[80,5120]{1,0:T(8,128)(2,1)} %collective-permute-done.2), channel_id=1, source_target_pairs={{0,1},{1,2},{2,3},{3,4},{4,5},{5,6},{6,7},{7,0},{8,9},{9,10},{10,1... | collective-permute-start | bytes 2457608 | tf_op jit(solution)/shard_map/ppermute | solution.py:102
  103.4 1.4 fusion.74
  104.8 1.7 compare_and_fusion
  106.5 16.3 %collective-permute-start.6 = (bf16[80,5120]{1,0:T(8,128)(2,1)}, bf16[80,5120]{1,0:T(8,128)(2,1)S(1)}, u32[]{:S(2)}, u32[]{:S(2)}) collective-permute-start(bf16[80,5120]{1,0:T(8,128)(2,1)} %collective-permute-done.5), channel_id=1, source_target_pairs={{0,7},{1,0},{2,1},{3,2},{4,3},{5,4},{6,5},{7,6},{8,15},{9,8},{10,9... | collective-permute-start | bytes 2457608 | tf_op jit(solution)/shard_map/ppermute | solution.py:103
  122.8 14.5 %collective-permute-done.3 = bf16[80,5120]{1,0:T(8,128)(2,1)} collective-permute-done((bf16[80,5120]{1,0:T(8,128)(2,1)}, bf16[80,5120]{1,0:T(8,128)(2,1)}, u32[]{:S(2)}, u32[]{:S(2)}) %collective-permute-start.3) | collective-permute-done | bytes 819232 | tf_op jit(solution)/shard_map/ppermute | solution.py:102
  137.3 8.5 %constant_dynamic-update-slice_fusion.15 = (f32[1280,3,512]{2,0,1:T(8,128)S(1)}, f32[80,3,512]{2,0,1:T(8,128)S(1)}) fusion(bf16[3,5120,512]{2,1,0:T(8,128)(2,1)} %param.12, bf16[80,5120]{1,0:T(8,128)(2,1)} %collective-permute-done.3), kind=kOutput, calls=%fused_computation.137 | convolution fusion | flops 1258291200 | bytes 17530880 | tf_op jit(solution)/shard_map/td,cdh->tch/dot_general | solution.py:96
  145.8 4.0 %constant_dynamic-update-slice_fusion.14 = (f32[1280,3,512]{2,0,1:T(8,128)S(1)}, f32[80,3,512]{2,0,1:T(8,128)S(1)}) fusion(f32[1280,3,512]{2,0,1:T(8,128)S(1)} %get-tuple-element.43, bf16[3,5120,512]{2,1,0:T(8,128)(2,1)S(1)} %bitcast.149, bf16[80,5120]{1,0:T(8,128)(2,1)} %collective-permute-done.2), kind=kOutput, calls=%fused_computation.136 | convolution fusion | flops 1258291200 | bytes 17530880 | tf_op jit(solution)/shard_map/td,cdh->tch/dot_general | solution.py:96
  149.9 2.9 %constant_dynamic-update-slice_fusion.13 = (f32[1280,3,512]{2,0,1:T(8,128)S(1)}, f32[80,3,512]{2,0,1:T(8,128)S(1)}) fusion(f32[1280,3,512]{2,0,1:T(8,128)S(1)} %get-tuple-element.45, bf16[3,5120,512]{2,1,0:T(8,128)(2,1)S(1)} %bitcast.149, bf16[80,5120]{1,0:T(8,128)(2,1)S(1)} %collective-permute-done.1), kind=kOutput, calls=%fused_computation.135 | convolution fusion | flops 1258291200 | bytes 17530880 | tf_op jit(solution)/shard_map/td,cdh->tch/dot_general | solution.py:96
  152.7 2.9 %constant_dynamic-update-slice_fusion.12 = (f32[1280,3,512]{2,0,1:T(8,128)S(1)}, f32[80,3,512]{2,0,1:T(8,128)S(1)}) fusion(f32[1280,3,512]{2,0,1:T(8,128)S(1)} %get-tuple-element.47, bf16[3,5120,512]{2,1,0:T(8,128)(2,1)S(1)} %bitcast.149, bf16[80,5120]{1,0:T(8,128)(2,1)S(1)} %collective-permute-done), kind=kOutput, calls=%fused_computation.134 | convolution fusion | flops 1258291200 | bytes 17530880 | tf_op jit(solution)/shard_map/td,cdh->tch/dot_general | solution.py:96
  155.6 2.9 %constant_dynamic-update-slice_fusion.11 = (f32[1280,3,512]{2,0,1:T(8,128)S(1)}, f32[80,3,512]{2,0,1:T(8,128)S(1)}) fusion(f32[1280,3,512]{2,0,1:T(8,128)S(1)} %get-tuple-element.49, bf16[3,5120,512]{2,1,0:T(8,128)(2,1)S(1)} %bitcast.149, bf16[80,5120]{1,0:T(8,128)(2,1)S(1)} %fusion.1), kind=kOutput, calls=%fused_computation.133 | convolution fusion | flops 1258291200 | bytes 17530880 | tf_op jit(solution)/shard_map/td,cdh->tch/dot_general | solution.py:96
  158.5 2.9 %constant_dynamic-update-slice_fusion.10 = (f32[1280,3,512]{2,0,1:T(8,128)S(1)}, f32[80,3,512]{2,0,1:T(8,128)S(1)}) fusion(f32[1280,3,512]{2,0,1:T(8,128)S(1)} %get-tuple-element.51, bf16[3,5120,512]{2,1,0:T(8,128)(2,1)S(1)} %bitcast.149, bf16[80,5120]{1,0:T(8,128)(2,1)S(1)} %collective-permute-done.4), kind=kOutput, calls=%fused_computation.132 | convolution fusion | flops 1258291200 | bytes 17530880 | tf_op jit(solution)/shard_map/td,cdh->tch/dot_general | solution.py:100
  161.4 4.2 %constant_dynamic-update-slice_fusion.9 = (f32[1280,3,512]{2,0,1:T(8,128)S(1)}, f32[80,3,512]{2,0,1:T(8,128)S(1)}) fusion(f32[1280,3,512]{2,0,1:T(8,128)S(1)} %get-tuple-element.53, bf16[3,5120,512]{2,1,0:T(8,128)(2,1)S(1)} %bitcast.149, bf16[80,5120]{1,0:T(8,128)(2,1)} %collective-permute-done.5), kind=kOutput, calls=%fused_computation.131 | convolution fusion | flops 1258291200 | bytes 17530880 | tf_op jit(solution)/shard_map/td,cdh->tch/dot_general | solution.py:100
  165.6 2.9 %constant_dynamic-update-slice_fusion.8 = (f32[1280,3,512]{2,0,1:T(8,128)S(1)}, f32[80,3,512]{2,0,1:T(8,128)S(1)}) fusion(f32[1280,3,512]{2,0,1:T(8,128)S(1)} %get-tuple-element.55, bf16[3,5120,512]{2,1,0:T(8,128)(2,1)S(1)} %bitcast.149, bf16[80,5120]{1,0:T(8,128)(2,1)S(1)} %collective-permute-done.6), kind=kOutput, calls=%fused_computation.130 | convolution fusion | flops 1258291200 | bytes 17530880 | tf_op jit(solution)/shard_map/td,cdh->tch/dot_general | solution.py:100
  168.8 1.7 multiply_reduce_fusion
  170.4 1.8 copy-done.3
  172.6 19.9 %all-reduce = (f32[640]{0:T(1024)S(1)}, f32[640]{0:T(1024)S(1)}) all-reduce(f32[640]{0:T(1024)S(1)} %get-tuple-element.11, f32[640]{0:T(1024)S(1)} %get-tuple-element.7), channel_id=1, replica_groups=mesh['rep'=4,'tp'=8] {'tp'}, use_global_device_ids=true, to_apply=%region_3.4 | all-reduce | flops 1280 | bytes 10240 | tf_op jit(solution)/shard_map/psum | solution.py:112
  192.7 1.6 slice.102
  194.3 1.6 slice.103
  195.8 1.7 copy.120
  198.1 1.5 slice.97
  201.6 1.5 dynamic-slice_convert_fusion
  217.2 3.5 %all-to-all-start = ((bf16[8,80,512]{2,1,0:T(8,128)(2,1)}), bf16[8,80,512]{2,1,0:T(8,128)(2,1)S(1)}, u32[]{:S(2)}, u32[]{:S(2)}) async-start(bf16[8,80,512]{2,1,0:T(8,128)(2,1)} %all_to_all.14), calls=%async_computation | async-start | bytes 1310720 | tf_op jit(solution)/shard_map/all_to_all | solution.py:129
  220.8 5.0 %convert_element_type.94 = bf16[1,40,16,4,128]{2,1,4,3,0:T(8,128)(2,1)} reshape(bf16[640,4,64,2]{0,3,2,1:T(2,128)(2,1)S(1)} %maximum_convert_fusion) | data formatting | bytes 1310720 | tf_op jit(solution)/shard_map/convert_element_type | solution.py:122
  226.0 4.6 %copy.112 = bf16[1,40,16,4,128]{4,2,3,1,0:T(8,128)(2,1)S(1)} copy(bf16[1,40,16,4,128]{2,1,4,3,0:T(8,128)(2,1)} %convert_element_type.94) | data formatting | bytes 1310720 | tf_op jit(solution)/shard_map/convert_element_type | solution.py:122
  233.0 5.6 %scatter_fusion = bf16[2,4,80,16,128]{4,3,2,1,0:T(8,128)(2,1)S(1)} fusion(bf16[2,4,80,16,128]{4,3,2,1,0:T(8,128)(2,1)S(1)} %copy-done.2, s32[40]{0:T(128)S(1)} %compare_select_fusion, bf16[40,2,4,16,128]{4,3,2,1,0:T(8,128)(2,1)} %copy.114), kind=kCustom, calls=%fused_computation | custom fusion | bytes 3932320 | tf_op jit(solution)/shard_map/scatter | solution.py:133
  (112 shorter events, 26.0 us)
Async XLA Ops:
  0.6 1.0 copy-start.6
  0.6 1.3 copy-start
  0.6 1.9 copy-start.11
  3.6 99.7 %copy-start.12 = (s32[3,640]{1,0:T(4,128)S(1)}, s32[3,640]{1,0:T(4,128)}, u32[]{:S(2)}) copy-start(s32[3,640]{1,0:T(4,128)} %param.16) | copy-start | bytes 23044
  3.6 99.7 %copy-start.13 = (f32[2,512]{1,0:T(2,128)S(1)}, f32[2,512]{1,0:T(2,128)}, u32[]{:S(2)}) copy-start(f32[2,512]{1,0:T(2,128)} %param.14) | copy-start | bytes 12292
  3.7 99.7 %copy-start.14 = (f32[64]{0:T(128)S(1)}, f32[64]{0:T(128)}, u32[]{:S(2)}) copy-start(f32[64]{0:T(128)} %constant.61.clone) | copy-start | bytes 772
  3.7 99.7 %copy-start.15 = (f32[64]{0:T(128)S(1)}, f32[64]{0:T(128)}, u32[]{:S(2)}) copy-start(f32[64]{0:T(128)} %constant.62.clone) | copy-start | bytes 772
  3.7 99.7 %copy-start.16 = (f32[64]{0:T(128)S(1)}, f32[64]{0:T(128)}, u32[]{:S(2)}) copy-start(f32[64]{0:T(128)} %constant.63.clone) | copy-start | bytes 772
  4.5 24.3 %collective-permute-start = (bf16[80,5120]{1,0:T(8,128)(2,1)S(1)}, bf16[80,5120]{1,0:T(8,128)(2,1)S(1)}, u32[]{:S(2)}, u32[]{:S(2)}) collective-permute-start(bf16[80,5120]{1,0:T(8,128)(2,1)S(1)} %fusion.1), channel_id=1, source_target_pairs={{0,1},{1,2},{2,3},{3,4},{4,5},{5,6},{6,7},{7,0},{8,9},{9,10},{10,1... | collective-permute-start | bytes 2457608 | tf_op jit(solution)/shard_map/ppermute | solution.py:102
  28.9 34.8 %collective-permute-start.1 = (bf16[80,5120]{1,0:T(8,128)(2,1)S(1)}, bf16[80,5120]{1,0:T(8,128)(2,1)S(1)}, u32[]{:S(2)}, u32[]{:S(2)}) collective-permute-start(bf16[80,5120]{1,0:T(8,128)(2,1)S(1)} %collective-permute-done), channel_id=1, source_target_pairs={{0,1},{1,2},{2,3},{3,4},{4,5},{5,6},{6,7},{7,0},{8,9},{9,10},{10,1... | collective-permute-start | bytes 2457608 | tf_op jit(solution)/shard_map/ppermute | solution.py:102
  28.9 37.3 %collective-permute-start.4 = (bf16[80,5120]{1,0:T(8,128)(2,1)S(1)}, bf16[80,5120]{1,0:T(8,128)(2,1)S(1)}, u32[]{:S(2)}, u32[]{:S(2)}) collective-permute-start(bf16[80,5120]{1,0:T(8,128)(2,1)S(1)} %fusion.1), channel_id=1, source_target_pairs={{0,7},{1,0},{2,1},{3,2},{4,3},{5,4},{6,5},{7,6},{8,15},{9,8},{10,9... | collective-permute-start | bytes 2457608 | tf_op jit(solution)/shard_map/ppermute | solution.py:103
  63.6 36.5 %collective-permute-start.2 = (bf16[80,5120]{1,0:T(8,128)(2,1)S(1)}, bf16[80,5120]{1,0:T(8,128)(2,1)}, u32[]{:S(2)}, u32[]{:S(2)}) collective-permute-start(bf16[80,5120]{1,0:T(8,128)(2,1)S(1)} %collective-permute-done.1), channel_id=1, source_target_pairs={{0,1},{1,2},{2,3},{3,4},{4,5},{5,6},{6,7},{7,0},{8,9},{9,10},{10,1... | collective-permute-start | bytes 2457608 | tf_op jit(solution)/shard_map/ppermute | solution.py:102
  66.1 40.4 %collective-permute-start.5 = (bf16[80,5120]{1,0:T(8,128)(2,1)S(1)}, bf16[80,5120]{1,0:T(8,128)(2,1)}, u32[]{:S(2)}, u32[]{:S(2)}) collective-permute-start(bf16[80,5120]{1,0:T(8,128)(2,1)S(1)} %collective-permute-done.4), channel_id=1, source_target_pairs={{0,7},{1,0},{2,1},{3,2},{4,3},{5,4},{6,5},{7,6},{8,15},{9,8},{10,9... | collective-permute-start | bytes 2457608 | tf_op jit(solution)/shard_map/ppermute | solution.py:103
  100.1 37.2 %collective-permute-start.3 = (bf16[80,5120]{1,0:T(8,128)(2,1)}, bf16[80,5120]{1,0:T(8,128)(2,1)}, u32[]{:S(2)}, u32[]{:S(2)}) collective-permute-start(bf16[80,5120]{1,0:T(8,128)(2,1)} %collective-permute-done.2), channel_id=1, source_target_pairs={{0,1},{1,2},{2,3},{3,4},{4,5},{5,6},{6,7},{7,0},{8,9},{9,10},{10,1... | collective-permute-start | bytes 2457608 | tf_op jit(solution)/shard_map/ppermute | solution.py:102
  103.4 42.4 %slice-start = ((s8[15728640]{0:T(1024)(128)(4,1)}), s8[4194304]{0:T(1024)(128)(4,1)S(1)}, s32[]{:S(2)}) async-start(s8[15728640]{0:T(1024)(128)(4,1)} %bitcast.148), calls=%async_computation.1 | async-start | bytes 8388608
  106.5 39.3 %slice-start.1 = ((s8[15728640]{0:T(1024)(128)(4,1)}), s8[4194304]{0:T(1024)(128)(4,1)S(1)}, s32[]{:S(2)}) async-start(s8[15728640]{0:T(1024)(128)(4,1)} %bitcast.148), calls=%async_computation.2 | async-start | bytes 8388608
  106.5 39.3 %slice-start.2 = ((s8[15728640]{0:T(1024)(128)(4,1)}), s8[4194304]{0:T(1024)(128)(4,1)S(1)}, s32[]{:S(2)}) async-start(s8[15728640]{0:T(1024)(128)(4,1)} %bitcast.148), calls=%async_computation.3 | async-start | bytes 8388608
  106.5 39.4 %slice-start.3 = ((s8[15728640]{0:T(1024)(128)(4,1)}), s8[3145728]{0:T(1024)(128)(4,1)S(1)}, s32[]{:S(2)}) async-start(s8[15728640]{0:T(1024)(128)(4,1)} %bitcast.148), calls=%async_computation.4 | async-start | bytes 6291456
  106.5 59.1 %collective-permute-start.6 = (bf16[80,5120]{1,0:T(8,128)(2,1)}, bf16[80,5120]{1,0:T(8,128)(2,1)S(1)}, u32[]{:S(2)}, u32[]{:S(2)}) collective-permute-start(bf16[80,5120]{1,0:T(8,128)(2,1)} %collective-permute-done.5), channel_id=1, source_target_pairs={{0,7},{1,0},{2,1},{3,2},{4,3},{5,4},{6,5},{7,6},{8,15},{9,8},{10,9... | collective-permute-start | bytes 2457608 | tf_op jit(solution)/shard_map/ppermute | solution.py:103
  168.8 3.5 %copy-start.3 = (f32[1280,3,512]{2,0,1:T(8,128)}, f32[1280,3,512]{2,0,1:T(8,128)S(1)}, u32[]{:S(2)}) copy-start(f32[1280,3,512]{2,0,1:T(8,128)S(1)} %constant_dynamic-update-slice_fusion) | copy-start | bytes 23592964
  197.7 1.9 copy-start.4
  197.7 1.9 copy-start.5
  207.7 0.9 copy-start.10
  208.6 0.9 copy-start.9
  209.6 0.9 copy-start.8
  210.5 0.9 copy-start.7
  216.2 4.6 %copy-start.17 = (s32[40]{0:T(128)S(1)}, s32[40]{0:T(128)}, u32[]{:S(2)}) copy-start(s32[40]{0:T(128)} %param.17) | copy-start | bytes 484
  217.2 21.4 %all-to-all-start = ((bf16[8,80,512]{2,1,0:T(8,128)(2,1)}), bf16[8,80,512]{2,1,0:T(8,128)(2,1)S(1)}, u32[]{:S(2)}, u32[]{:S(2)}) async-start(bf16[8,80,512]{2,1,0:T(8,128)(2,1)} %all_to_all.14), calls=%async_computation | async-start | bytes 1310720 | tf_op jit(solution)/shard_map/all_to_all | solution.py:129
  230.8 2.2 copy-start.2
  238.6 1.7 copy-start.1
